TPU v7x, 256 devices: a whole 4x4x8 slice. The times are simulated.
256 devices in a mesh: section: 8 (over y, core), dp: 32 (over z, x).
Axes of the slice: x: 4, y: 4, z: 8, core: 2. Of those that a mesh axis runs over, the one named last changes fastest.
Arguments:
- crop_maps: bfloat16 [32, 4, 2, 8, 8, 640], P('dp'), may hold values from -6 to 6
- target_maps: int32 [32, 4, 2, 8, 8], P('dp'), may hold values 0 or 1
- crop_counts: int32 [32, 4], P('dp'), may hold values from 1 to 2, as said below
- depth_kernels: float32 [8, 49, 640], P('section'), may hold values from -0.875 to 0.875
- weight_in: bfloat16 [8, 640, 2560], P('section', 'dp'), may hold values from -0.25 to 0.25
- weight_out: bfloat16 [8, 2560, 640], P('section', 'dp'), may hold values from -0.125 to 0.125
- head_weight: float32 [640], replicated, may hold values from -0.25 to 0.25
Outputs:
- grad_in: float32 [8, 640, 2560], P('section', 'dp')
- grad_out: float32 [8, 2560, 640], P('section', 'dp')
- grad_kernels: float32 [8, 49, 640], P('section')
- grad_head: float32 [640], replicated
- loss_value: float32 [], replicated
Inputs may be any that keep to these rules, and one draw needn't show every extreme that they name: `crop_counts`: every data group has some micro-batch with exactly 2 crops.
All inputs are finite; a program needn't handle non-finite values. No bound on the sum of `target_maps` on one device may be relied on, other than what follows from the above.
Results may differ from a plain program's by a relative error of at most 0.034.
Values may be sent and summed in bfloat16 or wider, within the bound.
No kernel may reach another device: no remote copies, remote signals or barrier semaphores. Data moves between devices by JAX's collectives and lax.ppermute only.
A program may use at most 128 MiB of HBM per device.

v0:
```python
import jax
import jax.numpy as jnp
from jax import lax
from jax.sharding import PartitionSpec as P

EPSILON = 1e-06
SQRT_HALF = 0.7071067811865476
INV_ROOT_TWO_PI = 0.3989422804014327


def from_behind(value, axis, steps):
    count = lax.axis_size(axis)
    first, last = (max(0, -steps), min(count, count - steps))
    return lax.ppermute(value, axis, [(source, source + steps) for source in range(first, last)])


def depthwise(values, kernel):
    side = values.shape[1]
    padded = jnp.pad(values, ((0, 0), (3, 3), (3, 3), (0, 0)))
    result = jnp.zeros_like(values)
    for vertical in range(7):
        for across in range(7):
            result = (
                result
                + padded[:, vertical : vertical + side, across : across + side, :]
                * kernel[vertical * 7 + across]
            )
    return result


def depthwise_back(grads, kernel):
    side = grads.shape[1]
    padded = jnp.pad(grads, ((0, 0), (3, 3), (3, 3), (0, 0)))
    result = jnp.zeros_like(grads)
    for vertical in range(7):
        for across in range(7):
            result = (
                result
                + padded[:, 6 - vertical : 6 - vertical + side, 6 - across : 6 - across + side, :]
                * kernel[vertical * 7 + across]
            )
    return result


def kernel_grad(values, grads):
    side = values.shape[1]
    padded = jnp.pad(values, ((0, 0), (3, 3), (3, 3), (0, 0)))
    taps = []
    for vertical in range(7):
        for across in range(7):
            taps.append(
                jnp.sum(
                    padded[:, vertical : vertical + side, across : across + side, :] * grads,
                    axis=(0, 1, 2),
                )
            )
    return jnp.stack(taps, axis=0)


def block_parts(tiles, kernel, weight_in):
    width = tiles.shape[-1]
    widened = tiles.astype(jnp.float32)
    mixed = depthwise(widened, kernel).reshape(-1, width)
    centred = mixed - jnp.mean(mixed, axis=-1, keepdims=True)
    inverse = lax.rsqrt(jnp.mean(centred * centred, axis=-1, keepdims=True) + EPSILON)
    normed = centred * inverse
    normed_low = normed.astype(jnp.bfloat16)
    hidden = jnp.dot(normed_low, weight_in, preferred_element_type=jnp.float32)
    activated = (hidden * 0.5 * (1.0 + lax.erf(hidden * SQRT_HALF))).astype(jnp.bfloat16)
    return (widened, normed, inverse, normed_low, hidden, activated)


def block_forward(tiles, kernel, weight_in, weight_out):
    width = tiles.shape[-1]
    widened, normed, inverse, normed_low, hidden, activated = block_parts(tiles, kernel, weight_in)
    output = jnp.dot(activated, weight_out, preferred_element_type=jnp.float32)
    return (widened.reshape(-1, width) + output).astype(jnp.bfloat16).reshape(tiles.shape)


def block_backward(tiles, upstream, kernel, weight_in, weight_out):
    width = tiles.shape[-1]
    widened, normed, inverse, normed_low, hidden, activated = block_parts(tiles, kernel, weight_in)
    up_flat = upstream.reshape(-1, width)
    through = lax.dot_general(
        up_flat, weight_out, (((1,), (1,)), ((), ())), preferred_element_type=jnp.float32
    )
    slope = (
        0.5 * (1.0 + lax.erf(hidden * SQRT_HALF))
        + hidden * jnp.exp(-0.5 * hidden * hidden) * INV_ROOT_TWO_PI
    )
    hidden_grad = (through * slope).astype(jnp.bfloat16)
    normed_grad = lax.dot_general(
        hidden_grad, weight_in, (((1,), (1,)), ((), ())), preferred_element_type=jnp.float32
    )
    mixed_grad = inverse * (
        normed_grad
        - jnp.mean(normed_grad, axis=-1, keepdims=True)
        - normed * jnp.mean(normed_grad * normed, axis=-1, keepdims=True)
    )
    mixed_tiles = mixed_grad.reshape(tiles.shape)
    kernel_term = kernel_grad(widened, mixed_tiles)
    tile_grad = (upstream.astype(jnp.float32) + depthwise_back(mixed_tiles, kernel)).astype(
        jnp.bfloat16
    )
    return (tile_grad, kernel_term, normed_low, hidden_grad, activated, up_flat)


def outer_sum(left, right):
    return lax.dot_general(
        left, right, (((0,), (0,)), ((), ())), preferred_element_type=jnp.float32
    )


def head_terms(final, targets, live, head_weight, factor):
    widened = final.astype(jnp.float32)
    logits = jnp.sum(widened * head_weight, axis=-1)
    weight_live = live.astype(jnp.float32)[:, :, None, None]
    truth = targets.astype(jnp.float32)
    loss_term = jnp.sum(weight_live * (jax.nn.softplus(logits) - truth * logits)) * factor
    logit_grad = (jax.nn.sigmoid(logits) - truth) * weight_live * factor
    seeds = (logit_grad[..., None] * head_weight).astype(jnp.bfloat16)
    head_term = jnp.sum(logit_grad[..., None] * widened, axis=(0, 1, 2, 3))
    return (loss_term, seeds, head_term)


def body(crop_maps, target_maps, crop_counts, depth_kernels, weight_in, weight_out, head_weight):
    section_index = lax.axis_index("section")
    section_count = lax.axis_size("section")
    micro_count = crop_maps.shape[1]
    slot_count = crop_maps.shape[2]
    kernel = depth_kernels[0]
    live = jnp.arange(slot_count)[None, :] < crop_counts[0][:, None]
    entering = crop_maps[0] * live[:, :, None, None, None].astype(jnp.bfloat16)
    first_full, second_full = (
        lax.all_gather(weight_in[0], "dp", axis=0, tiled=True),
        lax.all_gather(weight_out[0], "dp", axis=0, tiled=True),
    )
    blank_tile = jnp.zeros(entering.shape[1:], jnp.bfloat16)
    ticks = micro_count + section_count - 1

    def forward_step(moment, carry):
        arrived, saved, final = carry
        micro = moment - section_index
        active = (micro >= 0) & (micro < micro_count)
        place = jnp.clip(micro, 0, micro_count - 1)
        own_tiles = lax.dynamic_index_in_dim(entering, place, 0, keepdims=False)
        current = jnp.where(section_index == 0, own_tiles, arrived)
        result = lax.cond(
            active,
            lambda tiles: block_forward(tiles, kernel, first_full, second_full),
            lambda tiles: jnp.zeros_like(tiles),
            current,
        )
        old_saved = lax.dynamic_index_in_dim(saved, place, 0, keepdims=False)
        saved = lax.dynamic_update_index_in_dim(
            saved, jnp.where(active, current, old_saved), place, 0
        )
        old_final = lax.dynamic_index_in_dim(final, place, 0, keepdims=False)
        final = lax.dynamic_update_index_in_dim(
            final, jnp.where(active, result, old_final), place, 0
        )
        arrived = from_behind(result, "section", 1)
        return (arrived, saved, final)

    _, saved, final = lax.fori_loop(
        0, ticks, forward_step, (blank_tile, jnp.zeros_like(entering), jnp.zeros_like(entering))
    )
    is_last = section_index == section_count - 1
    last_weight = is_last.astype(jnp.float32)
    factor = 1.0 / (micro_count * slot_count)
    loss_term, seeds, head_term = head_terms(final, target_maps[0], live, head_weight, factor)
    head_total, loss_total = lax.psum(
        (head_term * last_weight, loss_term * last_weight), ("section", "dp")
    )
    first_back, second_back = (
        lax.all_gather(weight_in[0], "dp", axis=0, tiled=True),
        lax.all_gather(weight_out[0], "dp", axis=0, tiled=True),
    )
    width = entering.shape[-1]
    expand = first_back.shape[1]
    extra_start = (jnp.zeros((width, expand), jnp.float32), jnp.zeros((expand, width), jnp.float32))

    def backward_step(moment, carry):
        arrived, kernel_acc, extra = carry
        micro = moment - (section_count - 1 - section_index)
        active = (micro >= 0) & (micro < micro_count)
        place = jnp.clip(micro, 0, micro_count - 1)
        own_seed = lax.dynamic_index_in_dim(seeds, place, 0, keepdims=False)
        upstream = jnp.where(is_last, own_seed, arrived)
        stored = lax.dynamic_index_in_dim(saved, place, 0, keepdims=False)

        def run_block(operands):
            grad_tiles, inputs, acc_kernel, acc_extra = operands
            tile_grad, kernel_term, normed_low, hidden_grad, activated, up_flat = block_backward(
                inputs, grad_tiles, kernel, first_back, second_back
            )
            new_extra = (
                acc_extra[0] + outer_sum(normed_low, hidden_grad),
                acc_extra[1] + outer_sum(activated, up_flat),
            )
            return (tile_grad, acc_kernel + kernel_term, new_extra)

        def skip_block(operands):
            return (jnp.zeros_like(operands[0]), operands[2], operands[3])

        tile_grad, kernel_acc, extra = lax.cond(
            active, run_block, skip_block, (upstream, stored, kernel_acc, extra)
        )
        arrived = from_behind(tile_grad, "section", -1)
        return (arrived, kernel_acc, extra)

    _, kernel_acc, extra = lax.fori_loop(
        0, ticks, backward_step, (blank_tile, jnp.zeros(kernel.shape, jnp.float32), extra_start)
    )
    first_part, second_part = (
        lax.psum_scatter(
            extra[0].astype(jnp.bfloat16), "dp", scatter_dimension=0, tiled=True
        ).astype(jnp.float32),
        lax.psum_scatter(
            extra[1].astype(jnp.bfloat16), "dp", scatter_dimension=0, tiled=True
        ).astype(jnp.float32),
    )
    kernel_total = lax.psum(kernel_acc.astype(jnp.bfloat16), "dp").astype(jnp.float32)
    return (first_part[None], second_part[None], kernel_total[None], head_total, loss_total)


def solution(mesh):
    return jax.shard_map(
        body,
        mesh=mesh,
        in_specs=(
            P("dp", None, None, None, None, None),
            P("dp", None, None, None, None),
            P("dp", None),
            P("section", None, None),
            P("section", "dp", None),
            P("section", "dp", None),
            P(),
        ),
        out_specs=(
            P("section", "dp", None),
            P("section", "dp", None),
            P("section", None, None),
            P(),
            P(),
        ),
        check_vma=False,
    )
```

profile of v0, /device:TPU:1, one launch (start us, length us, event | category | flops | bytes accessed | tf_op | source)
XLA Modules:
  0.0 1533.0 jit_solution(5656709828315738469)
XLA Ops:
  13.1 91.3 %all-gather.5.cloned.1.call-done = bf16[1,640,2560]{2,0,1:T(2,128)(2,1)} async-done(((bf16[1,20,2560]{2,0,1:T(2,128)(2,1)}), bf16[1,640,2560]{2,0,1:T(2,128)(2,1)}) %all-gather.5.cloned.1.call-update) | async-done | bytes 3276816 | tf_op jit(solution)/shard_map/all_gather | solution.py:135
  104.4 3.6 copy.20
  108.0 72.7 %all-gather.7.cloned.1.call-done = bf16[1,2560,640]{2,1,0:T(8,128)(2,1)} async-done(((bf16[1,80,640]{2,1,0:T(8,128)(2,1)}), bf16[1,2560,640]{2,1,0:T(8,128)(2,1)}) %all-gather.7.cloned.1.call-update) | async-done | bytes 3276816 | tf_op jit(solution)/shard_map/all_gather | solution.py:136
  183.2 210.7 %while.40 = (s32[]{:T(128)}, bf16[2,8,8,640]{3,2,1,0:T(8,128)(2,1)}, bf16[4,2,8,8,640]{4,3,2,1,0:T(8,128)(2,1)}, bf16[4,2,8,8,640]{4,3,2,1,0:T(8,128)(2,1)}, s32...) while((s32[]{:T(128)}, ...), condition=%wide.region_5.6_spmd, body=%wide.region_0.5_spmd.sunk | while | flops 849510528 | bytes 13491009 | solution.py:165
  185.9 7.7 collective-permute-start
  195.4 12.2 collective-permute-done
  210.3 14.7 conditional.5
  215.8 2.9 fusion.228
  221.8 3.3 fusion.3
  231.9 14.7 conditional.5
  237.4 2.9 fusion.228
  243.4 3.3 fusion.3
  246.6 4.5 collective-permute-start
  256.1 14.7 conditional.5
  261.6 2.9 fusion.228
  267.5 3.3 fusion.3
  270.8 4.5 collective-permute-start
  280.3 14.7 conditional.5
  285.8 2.9 fusion.228
  291.7 3.3 fusion.3
  295.0 4.5 collective-permute-start
  304.5 19.2 %collective-permute-start = (bf16[2,8,8,640]{3,2,1,0:T(8,128)(2,1)S(1)}, bf16[2,8,8,640]{3,2,1,0:T(8,128)(2,1)}, u32[]{:S(2)}, u32[]{:S(2)}) collective-permute-start(bf16[2,8,8,640]{3,2,1,0:T(8,128)(2,1)S(1)} %get-tuple-element.1153), channel_id=1, source_target_pairs={{0,32},{32,64},{64,96},{96,128},{128,160},{160,192},{192,224},{1,3... | collective-permute-start | bytes 491528 | tf_op jit(solution)/shard_map/while/body/eval_jaxpr/ppermute | solution.py:14
  328.7 4.5 collective-permute-start
  338.2 12.7 collective-permute-start
  355.9 4.5 collective-permute-start
  365.5 16.6 %collective-permute-start = (bf16[2,8,8,640]{3,2,1,0:T(8,128)(2,1)S(1)}, bf16[2,8,8,640]{3,2,1,0:T(8,128)(2,1)}, u32[]{:S(2)}, u32[]{:S(2)}) collective-permute-start(bf16[2,8,8,640]{3,2,1,0:T(8,128)(2,1)S(1)} %get-tuple-element.1153), channel_id=1, source_target_pairs={{0,32},{32,64},{64,96},{96,128},{128,160},{160,192},{192,224},{1,3... | collective-permute-start | bytes 491528 | tf_op jit(solution)/shard_map/while/body/eval_jaxpr/ppermute | solution.py:14
  387.1 4.5 collective-permute-start
  396.5 3.1 broadcast_in_dim.59
  399.7 3.5 broadcast_in_dim.58
  403.2 778.2 %while.41 = (s32[]{:T(128)}, bf16[2,8,8,640]{3,2,1,0:T(8,128)(2,1)}, f32[49,640]{1,0:T(8,128)S(1)}, f32[640,2560]{1,0:T(8,128)}, f32[2560,640]{1,0:T(8,128)}, /*...) while((s32[]{:T(128)}, ...), condition=%wide.region_63.64_spmd.clone, body=%wide.region_7.63_spmd.clone.sunk | while | flops 2131804288 | bytes 130983528 | solution.py:212
  407.5 14.1 collective-permute-done.1
  425.9 5.0 collective-permute-done.1
  435.2 17.3 %collective-permute-done.1 = bf16[2,8,8,640]{3,2,1,0:T(8,128)(2,1)} collective-permute-done((bf16[2,8,8,640]{3,2,1,0:T(8,128)(2,1)}, bf16[2,8,8,640]{3,2,1,0:T(8,128)(2,1)}, u32[]{:S(2)}, u32[]{:S(2)}) %collective-permute-start.1) | collective-permute-done | bytes 163872 | tf_op jit(solution)/shard_map/while/body/eval_jaxpr/ppermute | solution.py:14
  456.8 5.0 collective-permute-done.1
  466.1 13.4 collective-permute-done.1
  483.8 359.0 %collective-permute-done.1 = bf16[2,8,8,640]{3,2,1,0:T(8,128)(2,1)} collective-permute-done((bf16[2,8,8,640]{3,2,1,0:T(8,128)(2,1)}, bf16[2,8,8,640]{3,2,1,0:T(8,128)(2,1)}, u32[]{:S(2)}, u32[]{:S(2)}) %collective-permute-start.1) | collective-permute-done | bytes 163872 | tf_op jit(solution)/shard_map/while/body/eval_jaxpr/ppermute | solution.py:14
  844.6 60.5 %conditional.6 = (bf16[2,8,8,640]{3,2,1,0:T(8,128)(2,1)}, f32[49,640]{1,0:T(8,128)S(1)}, f32[640,2560]{1,0:T(8,128)}, f32[2560,640]{1,0:T(8,128)}) conditional(s32[]{:T(128)} %convert_element_type.175, (f32[49,640]{1,0:T(8,128)S(1)}, f32[640,2560]{1,0:T(8,128)}, f32[2560,640]{1,0:T(8,128)}) %tuple.251, (pred[]{:T(512)}, s32[]{:T(128)}, ...), branch_computations={%region_8.8_spmd, %region_9.62_spmd} | conditional | flops 2131148928 | bytes 129667864 | solution.py:206
  848.7 2.9 fusion.230
  884.0 8.0 stack.299
  893.8 7.2 convolution_add_fusion.1
  902.3 2.7 copy-done
  906.9 5.0 collective-permute-done.1
  913.7 60.5 %conditional.6 = (bf16[2,8,8,640]{3,2,1,0:T(8,128)(2,1)}, f32[49,640]{1,0:T(8,128)S(1)}, f32[640,2560]{1,0:T(8,128)}, f32[2560,640]{1,0:T(8,128)}) conditional(s32[]{:T(128)} %convert_element_type.175, (f32[49,640]{1,0:T(8,128)S(1)}, f32[640,2560]{1,0:T(8,128)}, f32[2560,640]{1,0:T(8,128)}) %tuple.251, (pred[]{:T(512)}, s32[]{:T(128)}, ...), branch_computations={%region_8.8_spmd, %region_9.62_spmd} | conditional | flops 2131148928 | bytes 129667864 | solution.py:206
  917.8 2.9 fusion.230
  953.1 8.0 stack.299
  962.9 7.2 convolution_add_fusion.1
  976.0 5.0 collective-permute-done.1
  982.8 60.5 %conditional.6 = (bf16[2,8,8,640]{3,2,1,0:T(8,128)(2,1)}, f32[49,640]{1,0:T(8,128)S(1)}, f32[640,2560]{1,0:T(8,128)}, f32[2560,640]{1,0:T(8,128)}) conditional(s32[]{:T(128)} %convert_element_type.175, (f32[49,640]{1,0:T(8,128)S(1)}, f32[640,2560]{1,0:T(8,128)}, f32[2560,640]{1,0:T(8,128)}) %tuple.251, (pred[]{:T(512)}, s32[]{:T(128)}, ...), branch_computations={%region_8.8_spmd, %region_9.62_spmd} | conditional | flops 2131148928 | bytes 129667864 | solution.py:206
  986.9 2.9 fusion.230
  1022.2 8.0 stack.299
  1032.0 7.2 convolution_add_fusion.1
  1045.1 5.0 collective-permute-done.1
  1051.9 60.5 %conditional.6 = (bf16[2,8,8,640]{3,2,1,0:T(8,128)(2,1)}, f32[49,640]{1,0:T(8,128)S(1)}, f32[640,2560]{1,0:T(8,128)}, f32[2560,640]{1,0:T(8,128)}) conditional(s32[]{:T(128)} %convert_element_type.175, (f32[49,640]{1,0:T(8,128)S(1)}, f32[640,2560]{1,0:T(8,128)}, f32[2560,640]{1,0:T(8,128)}) %tuple.251, (pred[]{:T(512)}, s32[]{:T(128)}, ...), branch_computations={%region_8.8_spmd, %region_9.62_spmd} | conditional | flops 2131148928 | bytes 129667864 | solution.py:206
  1056.0 2.9 fusion.230
  1091.3 8.0 stack.299
  1101.1 7.2 convolution_add_fusion.1
  1114.2 5.0 collective-permute-done.1
  1121.6 58.4 %collective-permute-start.1 = (bf16[2,8,8,640]{3,2,1,0:T(8,128)(2,1)}, bf16[2,8,8,640]{3,2,1,0:T(8,128)(2,1)}, u32[]{:S(2)}, u32[]{:S(2)}) collective-permute-start(bf16[2,8,8,640]{3,2,1,0:T(8,128)(2,1)} %get-tuple-element.1051), channel_id=1, source_target_pairs={{32,0},{64,32},{96,64},{128,96},{160,128},{192,160},{224,192},{33,... | collective-permute-start | bytes 491528 | tf_op jit(solution)/shard_map/while/body/eval_jaxpr/ppermute | solution.py:14
  1181.3 4.9 convert_element_type.134
  1188.1 3.2 convert_element_type.133
  1191.4 84.2 %fusion.2 = bf16[24,2560]{1,0:T(8,128)(2,1)} fusion(bf16[640,2560]{1,0:T(8,128)(2,1)S(1)} %convert_element_type.133), kind=kCustom, calls=%all-reduce-scatter | all-reduce-scatter fusion | flops 1966081 | bytes 3400704
  1283.4 9.5 collective-permute-start.7
  1294.3 110.5 %psum.21 = bf16[1,49,640]{2,0,1:T(2,128)(2,1)S(1)} all-reduce(bf16[1,49,640]{2,0,1:T(2,128)(2,1)S(1)} %broadcast_in_dim.64), channel_id=1, replica_groups=mesh['section'=8,'dp'=32] {'dp'}, use_global_device_ids=true, to_apply=%region_66.67 | all-reduce | flops 31360 | bytes 125440 | tf_op jit(solution)/shard_map/psum | solution.py:223
  1406.9 115.7 %all-reduce.5 = (f32[640]{0:T(1024)}, f32[]{:T(128)}) all-reduce(f32[640]{0:T(1024)S(1)} %broadcast_multiply_fusion.4, f32[]{:T(128)S(6)} %mul.2377), channel_id=1, replica_groups=mesh['section'=8,'dp'=32] {'section','dp'}, use_global_device_ids=true, to_apply=%region_68.69 | all-reduce | flops 641 | bytes 5128 | tf_op jit(solution)/shard_map/psum | solution.py:172
  (1136 shorter events, 327.4 us)
Async XLA Ops:
  7.2 5.0 copy-start.76
  7.2 97.2 %all-gather.5.cloned.1.call-start = ((), (), s32[]{:S(2)}) async-start(), calls=%async_computation.2 | async-start | bytes 6758400 | tf_op jit(solution)/shard_map/all_gather | solution.py:135
  9.0 171.6 %all-gather.7.cloned.1.call-start = ((), (), s32[]{:S(2)}) async-start(), calls=%async_computation.3 | async-start | bytes 3379200 | tf_op jit(solution)/shard_map/all_gather | solution.py:136
  9.8 1515.1 %reduce-scatter.4.cloned.1.call-start = ((), (), s32[]{:S(2)}) async-start(), calls=%async_computation.1 | async-start | bytes 3379200 | tf_op jit(solution)/shard_map/reduce_scatter | solution.py:219
  183.2 212.0 %copy-start.81 = (s32[1,4,2,8,8]{4,3,2,1,0:T(8,128)S(1)}, s32[1,4,2,8,8]{4,3,2,1,0:T(8,128)}, u32[]{:S(2)}) copy-start(s32[1,4,2,8,8]{4,3,2,1,0:T(8,128)} %param.16) | copy-start | bytes 6148
  185.9 21.6 %collective-permute-start = (bf16[2,8,8,640]{3,2,1,0:T(8,128)(2,1)S(1)}, bf16[2,8,8,640]{3,2,1,0:T(8,128)(2,1)}, u32[]{:S(2)}, u32[]{:S(2)}) collective-permute-start(bf16[2,8,8,640]{3,2,1,0:T(8,128)(2,1)S(1)} %get-tuple-element.1153), channel_id=1, source_target_pairs={{0,32},{32,64},{64,96},{96,128},{128,160},{160,192},{192,224},{1,3... | collective-permute-start | bytes 491528 | tf_op jit(solution)/shard_map/while/body/eval_jaxpr/ppermute | solution.py:14
  225.0 4.2 collective-permute-start
  246.6 6.8 collective-permute-start
  270.8 6.7 collective-permute-start
  295.0 6.7 collective-permute-start
  304.5 21.4 %collective-permute-start = (bf16[2,8,8,640]{3,2,1,0:T(8,128)(2,1)S(1)}, bf16[2,8,8,640]{3,2,1,0:T(8,128)(2,1)}, u32[]{:S(2)}, u32[]{:S(2)}) collective-permute-start(bf16[2,8,8,640]{3,2,1,0:T(8,128)(2,1)S(1)} %get-tuple-element.1153), channel_id=1, source_target_pairs={{0,32},{32,64},{64,96},{96,128},{128,160},{160,192},{192,224},{1,3... | collective-permute-start | bytes 491528 | tf_op jit(solution)/shard_map/while/body/eval_jaxpr/ppermute | solution.py:14
  328.7 6.7 collective-permute-start
  338.2 14.9 collective-permute-start
  355.9 6.7 collective-permute-start
  365.5 18.8 %collective-permute-start = (bf16[2,8,8,640]{3,2,1,0:T(8,128)(2,1)S(1)}, bf16[2,8,8,640]{3,2,1,0:T(8,128)(2,1)}, u32[]{:S(2)}, u32[]{:S(2)}) collective-permute-start(bf16[2,8,8,640]{3,2,1,0:T(8,128)(2,1)S(1)} %get-tuple-element.1153), channel_id=1, source_target_pairs={{0,32},{32,64},{64,96},{96,128},{128,160},{160,192},{192,224},{1,3... | collective-permute-start | bytes 491528 | tf_op jit(solution)/shard_map/while/body/eval_jaxpr/ppermute | solution.py:14
  387.1 6.7 collective-permute-start
  405.6 16.0 %collective-permute-start.1 = (bf16[2,8,8,640]{3,2,1,0:T(8,128)(2,1)}, bf16[2,8,8,640]{3,2,1,0:T(8,128)(2,1)}, u32[]{:S(2)}, u32[]{:S(2)}) collective-permute-start(bf16[2,8,8,640]{3,2,1,0:T(8,128)(2,1)} %get-tuple-element.1051), channel_id=1, source_target_pairs={{32,0},{64,32},{96,64},{128,96},{160,128},{192,160},{224,192},{33,... | collective-permute-start | bytes 491528 | tf_op jit(solution)/shard_map/while/body/eval_jaxpr/ppermute | solution.py:14
  423.9 6.9 collective-permute-start.1
  433.3 19.2 %collective-permute-start.1 = (bf16[2,8,8,640]{3,2,1,0:T(8,128)(2,1)}, bf16[2,8,8,640]{3,2,1,0:T(8,128)(2,1)}, u32[]{:S(2)}, u32[]{:S(2)}) collective-permute-start(bf16[2,8,8,640]{3,2,1,0:T(8,128)(2,1)} %get-tuple-element.1051), channel_id=1, source_target_pairs={{32,0},{64,32},{96,64},{128,96},{160,128},{192,160},{224,192},{33,... | collective-permute-start | bytes 491528 | tf_op jit(solution)/shard_map/while/body/eval_jaxpr/ppermute | solution.py:14
  454.9 6.9 collective-permute-start.1
  464.2 15.3 %collective-permute-start.1 = (bf16[2,8,8,640]{3,2,1,0:T(8,128)(2,1)}, bf16[2,8,8,640]{3,2,1,0:T(8,128)(2,1)}, u32[]{:S(2)}, u32[]{:S(2)}) collective-permute-start(bf16[2,8,8,640]{3,2,1,0:T(8,128)(2,1)} %get-tuple-element.1051), channel_id=1, source_target_pairs={{32,0},{64,32},{96,64},{128,96},{160,128},{192,160},{224,192},{33,... | collective-permute-start | bytes 491528 | tf_op jit(solution)/shard_map/while/body/eval_jaxpr/ppermute | solution.py:14
  481.9 361.0 %collective-permute-start.1 = (bf16[2,8,8,640]{3,2,1,0:T(8,128)(2,1)}, bf16[2,8,8,640]{3,2,1,0:T(8,128)(2,1)}, u32[]{:S(2)}, u32[]{:S(2)}) collective-permute-start(bf16[2,8,8,640]{3,2,1,0:T(8,128)(2,1)} %get-tuple-element.1051), channel_id=1, source_target_pairs={{32,0},{64,32},{96,64},{128,96},{160,128},{192,160},{224,192},{33,... | collective-permute-start | bytes 491528 | tf_op jit(solution)/shard_map/while/body/eval_jaxpr/ppermute | solution.py:14
  848.2 3.5 copy-start.14
  860.9 3.7 copy-start.3
  864.6 19.4 %copy-start.78 = (f32[1,640]{1,0:T(1,128)S(1)}, f32[1,640]{1,0:T(1,128)}, u32[]{:S(2)}) copy-start(f32[1,640]{1,0:T(1,128)} %stack.274) | copy-start | bytes 7684 | tf_op jit(solution)/shard_map/while/body/eval_jaxpr/cond
  892.0 9.0 slice-start
  893.8 7.2 slice-start.1
  893.8 7.2 copy-start.6
  893.8 7.2 copy-start.8
  901.0 4.1 copy-start.13
  905.0 6.9 collective-permute-start.1
  930.0 3.7 copy-start.3
  933.7 19.4 %copy-start.78 = (f32[1,640]{1,0:T(1,128)S(1)}, f32[1,640]{1,0:T(1,128)}, u32[]{:S(2)}) copy-start(f32[1,640]{1,0:T(1,128)} %stack.274) | copy-start | bytes 7684 | tf_op jit(solution)/shard_map/while/body/eval_jaxpr/cond
  961.1 9.0 slice-start
  962.9 7.2 slice-start.1
  962.9 7.2 copy-start.6
  962.9 7.2 copy-start.8
  970.1 4.1 copy-start.13
  974.1 6.9 collective-permute-start.1
  986.4 3.5 copy-start.14
  999.1 3.7 copy-start.3
  1002.8 19.4 %copy-start.78 = (f32[1,640]{1,0:T(1,128)S(1)}, f32[1,640]{1,0:T(1,128)}, u32[]{:S(2)}) copy-start(f32[1,640]{1,0:T(1,128)} %stack.274) | copy-start | bytes 7684 | tf_op jit(solution)/shard_map/while/body/eval_jaxpr/cond
  1030.2 9.0 slice-start
  1032.0 7.2 slice-start.1
  1032.0 7.2 copy-start.6
  1032.0 7.2 copy-start.8
  1039.1 4.1 copy-start.13
  1043.2 6.9 collective-permute-start.1
  1068.2 3.7 copy-start.3
  1071.9 19.4 %copy-start.78 = (f32[1,640]{1,0:T(1,128)S(1)}, f32[1,640]{1,0:T(1,128)}, u32[]{:S(2)}) copy-start(f32[1,640]{1,0:T(1,128)} %stack.274) | copy-start | bytes 7684 | tf_op jit(solution)/shard_map/while/body/eval_jaxpr/cond
  1099.2 9.0 slice-start
  1101.0 7.2 slice-start.1
  1101.0 7.2 copy-start.6
  1101.1 7.2 copy-start.8
  1108.2 4.1 copy-start.13
  1112.3 6.9 collective-permute-start.1
  1121.6 59.7 %collective-permute-start.1 = (bf16[2,8,8,640]{3,2,1,0:T(8,128)(2,1)}, bf16[2,8,8,640]{3,2,1,0:T(8,128)(2,1)}, u32[]{:S(2)}, u32[]{:S(2)}) collective-permute-start(bf16[2,8,8,640]{3,2,1,0:T(8,128)(2,1)} %get-tuple-element.1051), channel_id=1, source_target_pairs={{32,0},{64,32},{96,64},{128,96},{160,128},{192,160},{224,192},{33,... | collective-permute-start | bytes 491528 | tf_op jit(solution)/shard_map/while/body/eval_jaxpr/ppermute | solution.py:14
  1275.6 130.0 %copy-start.77 = (bf16[24,2560]{1,0:T(8,128)(2,1)S(1)}, bf16[24,2560]{1,0:T(8,128)(2,1)}, u32[]{:S(2)}) copy-start(bf16[24,2560]{1,0:T(8,128)(2,1)} %fusion.2) | copy-start | bytes 368644
  1276.5 246.1 %collective-permute-start.6 = (bf16[24,2560]{1,0:T(8,128)(2,1)}, bf16[24,2560]{1,0:T(8,128)(2,1)S(1)}, u32[]{:S(2)}, u32[]{:S(2)}) collective-permute-start(bf16[24,2560]{1,0:T(8,128)(2,1)} %fusion.2), channel_id=1, source_target_pairs={{0,5},{1,6},{2,7},{3,8},{4,9},{5,10},{6,11},{7,12},{8,13},{9,14},{... | collective-permute-start | bytes 368648
  1277.8 244.8 %collective-permute-start.5 = (bf16[24,2560]{1,0:T(8,128)(2,1)}, bf16[24,2560]{1,0:T(8,128)(2,1)S(1)}, u32[]{:S(2)}, u32[]{:S(2)}) collective-permute-start(bf16[24,2560]{1,0:T(8,128)(2,1)} %fusion.2), channel_id=1, source_target_pairs={{0,4},{1,5},{2,6},{3,7},{4,8},{5,9},{6,10},{7,11},{8,12},{9,13},{1... | collective-permute-start | bytes 368648
  1279.3 243.3 %collective-permute-start.4 = (bf16[24,2560]{1,0:T(8,128)(2,1)}, bf16[24,2560]{1,0:T(8,128)(2,1)S(1)}, u32[]{:S(2)}, u32[]{:S(2)}) collective-permute-start(bf16[24,2560]{1,0:T(8,128)(2,1)} %fusion.2), channel_id=1, source_target_pairs={{0,3},{1,4},{2,5},{3,6},{4,7},{5,8},{6,9},{7,10},{8,11},{9,12},{10... | collective-permute-start | bytes 368648
  1280.6 242.0 %collective-permute-start.3 = (bf16[24,2560]{1,0:T(8,128)(2,1)}, bf16[24,2560]{1,0:T(8,128)(2,1)S(1)}, u32[]{:S(2)}, u32[]{:S(2)}) collective-permute-start(bf16[24,2560]{1,0:T(8,128)(2,1)} %fusion.2), channel_id=1, source_target_pairs={{0,2},{1,3},{2,4},{3,5},{4,6},{5,7},{6,8},{7,9},{8,10},{9,11},{10,... | collective-permute-start | bytes 368648
  1283.4 122.2 %collective-permute-start.7 = (bf16[4,2560]{1,0:T(4,128)(2,1)S(1)}, bf16[4,2560]{1,0:T(4,128)(2,1)S(1)}, u32[]{:S(2)}, u32[]{:S(2)}) collective-permute-start(bf16[4,2560]{1,0:T(4,128)(2,1)S(1)} %slice.1262), channel_id=1, source_target_pairs={{0,6},{1,7},{2,8},{3,9},{4,10},{5,11},{6,12},{7,13},{8,14},{9,15},... | collective-permute-start | bytes 61448
  1405.6 117.0 %collective-permute-start.2 = (bf16[24,2560]{1,0:T(8,128)(2,1)S(1)}, bf16[24,2560]{1,0:T(8,128)(2,1)S(1)}, u32[]{:S(2)}, u32[]{:S(2)}) collective-permute-start(bf16[24,2560]{1,0:T(8,128)(2,1)S(1)} %copy-done.77), channel_id=1, source_target_pairs={{0,1},{1,2},{2,3},{3,4},{4,5},{5,6},{6,7},{7,8},{8,9},{9,10},{10,1... | collective-permute-start | bytes 368648
  (299 other events, 619.8 us)
Sparse Core Ops, SparseCore 0:
  11.2 93.1 all-gather.4
  107.0 73.6 all-gather.6
  1186.4 193.5 reduce-scatter.3
where the time goes:
time: 1540 us; the launch traced here: 1530 us
  waiting for transfers between devices  618 us (40%)
  blocking collectives  310 us (20%)
  local copies, waits for them, and re-layouts  199 us (13%)
  starting transfers between devices  180 us (12%)
  other arithmetic  145 us (9%)
  matrix products  59.4 us (4%)
    ppermute x22, waiting for transfers between devices, from_behind(): lax.ppermute(value, axis, [(source, source + steps) for source in range(f...  453 us
    ppermute x22, starting transfers between devices, from_behind(): lax.ppermute(value, axis, [(source, source + steps) for source in range(f...  163 us
    psum x1, blocking collectives, body(): lax.psum((head_term * last_weight, loss_term * last_weight), ('section',...  116 us
    psum x1, blocking collectives, body(): lax.psum(kernel_acc.astype(jnp.bfloat16), 'dp').astype(jnp.float32)  111 us
    another operation x200, local copies, waits for them, and re-layouts, kernel_grad(): return jnp.stack(taps, axis=0)  105 us
    all_gather x1, waiting for transfers between devices, body(): lax.all_gather(weight_in[0], 'dp', axis=0, tiled=True)  91.3 us
    unnamed x1, blocking collectives  84.2 us
    all_gather x1, waiting for transfers between devices, body(): lax.all_gather(weight_out[0], 'dp', axis=0, tiled=True)  72.7 us
  transfers between devices with their start and end apart: 31, of which 24 were waited for; matrix products, arithmetic and copies ran while one was open for 8% of the time, Pallas kernels for 0%

commit v1 on v0

--- a/solution.py
+++ b/solution.py
@@ -1,3 +1,4 @@
+import functools
 import jax
 import jax.numpy as jnp
 from jax import lax
@@ -6,6 +7,13 @@
 EPSILON = 1e-06
 SQRT_HALF = 0.7071067811865476
 INV_ROOT_TWO_PI = 0.3989422804014327
+
+
+def switch_tails(x_local, mesh_dim):
+    return jnp.sum(lax.all_gather(x_local, mesh_dim), axis=0)
+
+
+follow_table_for = functools.partial(switch_tails, mesh_dim="dp")
 
 
 def from_behind(value, axis, steps):
@@ -220,7 +228,7 @@
             extra[1].astype(jnp.bfloat16), "dp", scatter_dimension=0, tiled=True
         ).astype(jnp.float32),
     )
-    kernel_total = lax.psum(kernel_acc.astype(jnp.bfloat16), "dp").astype(jnp.float32)
+    kernel_total = follow_table_for(kernel_acc.astype(jnp.bfloat16)).astype(jnp.float32)
     return (first_part[None], second_part[None], kernel_total[None], head_total, loss_total)
 
 

time: 1540 us -> 1470 us (0.955)
  blocking collectives: 310 us -> 167 us
  waiting for transfers between devices: 618 us -> 687 us
    psum x1 -> x0, blocking collectives: 111 us -> none  [body(): lax.psum(kernel_acc.astype(jnp.bfloat16), 'dp').astype(jnp.float32)]
    reduce_scatter x1, waiting for transfers between devices: 0.01 us -> 69 us  [body(): lax.psum_scatter(extra[1].astype(jnp.bfloat16), 'dp', scatter_dimension=0...]
    psum x1, blocking collectives: 116 us -> 85.4 us  [body(): lax.psum((head_term * last_weight, loss_term * last_weight), ('section',...]
  transfers between devices with their start and end apart: 31 -> 32, of which waited for: 24 -> 25; matrix products, arithmetic and copies ran while one was open for 8% -> 8% of each run, Pallas kernels for 0% -> 0%
where the time goes in v1:
time: 1470 us; the launch traced here: 1460 us
  waiting for transfers between devices  687 us (47%)
  local copies, waits for them, and re-layouts  199 us (14%)
  starting transfers between devices  183 us (12%)
  blocking collectives  167 us (11%)
  other arithmetic  147 us (10%)
  matrix products  59.4 us (4%)
  between operations  15.2 us (1%)
    ppermute x22, waiting for transfers between devices, from_behind(): lax.ppermute(value, axis, [(source, source + steps) for source in range(f...  453 us
    ppermute x22, starting transfers between devices, from_behind(): lax.ppermute(value, axis, [(source, source + steps) for source in range(f...  163 us
    another operation x200, local copies, waits for them, and re-layouts, kernel_grad(): return jnp.stack(taps, axis=0)  105 us
    all_gather x1, waiting for transfers between devices, body(): lax.all_gather(weight_in[0], 'dp', axis=0, tiled=True)  91.3 us
    psum x1, blocking collectives, body(): lax.psum((head_term * last_weight, loss_term * last_weight), ('section',...  85.4 us
    unnamed x1, blocking collectives  81.5 us
    all_gather x1, waiting for transfers between devices, body(): lax.all_gather(weight_out[0], 'dp', axis=0, tiled=True)  72.7 us
    reduce_scatter x1, waiting for transfers between devices, body(): lax.psum_scatter(extra[1].astype(jnp.bfloat16), 'dp', scatter_dimension=0...  69 us
  transfers between devices with their start and end apart: 32, of which 25 were waited for; matrix products, arithmetic and copies ran while one was open for 8% of the time, Pallas kernels for 0%

profile of v1, /device:TPU:1, one launch (start us, length us, event | category | flops | bytes accessed | tf_op | source)
XLA Modules:
  0.0 1463.8 jit_solution(2081399517478236099)
XLA Ops:
  13.1 91.3 %all-gather.8.cloned.1.call-done = bf16[1,640,2560]{2,0,1:T(2,128)(2,1)} async-done(((bf16[1,20,2560]{2,0,1:T(2,128)(2,1)}), bf16[1,640,2560]{2,0,1:T(2,128)(2,1)}) %all-gather.8.cloned.1.call-update) | async-done | bytes 3276816 | tf_op jit(solution)/shard_map/all_gather | solution.py:143
  104.4 3.6 copy.20
  108.0 72.7 %all-gather.10.cloned.1.call-done = bf16[1,2560,640]{2,1,0:T(8,128)(2,1)} async-done(((bf16[1,80,640]{2,1,0:T(8,128)(2,1)}), bf16[1,2560,640]{2,1,0:T(8,128)(2,1)}) %all-gather.10.cloned.1.call-update) | async-done | bytes 3276816 | tf_op jit(solution)/shard_map/all_gather | solution.py:144
  183.2 210.7 %while.40 = (s32[]{:T(128)}, bf16[2,8,8,640]{3,2,1,0:T(8,128)(2,1)}, bf16[4,2,8,8,640]{4,3,2,1,0:T(8,128)(2,1)}, bf16[4,2,8,8,640]{4,3,2,1,0:T(8,128)(2,1)}, s32...) while((s32[]{:T(128)}, ...), condition=%wide.region_5.6_spmd, body=%wide.region_0.5_spmd.sunk | while | flops 849510528 | bytes 13491009 | solution.py:173
  185.9 7.7 collective-permute-start
  195.4 12.2 collective-permute-done
  210.3 14.7 %conditional.5 = (bf16[2,8,8,640]{3,2,1,0:T(8,128)(2,1)S(1)}) conditional(s32[]{:T(128)} %convert_element_type.191, () %tuple.248, (bf16[2,8,8,640]{3,2,1,0:T(8,128)(2,1)}, f32[49,640]{1,0:T(8,128)}, bf16[640,2560]{1,0:T(8,128)(2,1)S(1)}, bf16[2560,640]{1,0:T(8,128)(2,1)}) %tuple.249), branch_computations={%region_1.1_spmd, %region_2.4_spmd} | conditional | flops 849264768 | bytes 10868772 | solution.py:156
  215.8 2.9 fusion.228
  221.8 3.3 fusion.3
  231.9 14.7 %conditional.5 = (bf16[2,8,8,640]{3,2,1,0:T(8,128)(2,1)S(1)}) conditional(s32[]{:T(128)} %convert_element_type.191, () %tuple.248, (bf16[2,8,8,640]{3,2,1,0:T(8,128)(2,1)}, f32[49,640]{1,0:T(8,128)}, bf16[640,2560]{1,0:T(8,128)(2,1)S(1)}, bf16[2560,640]{1,0:T(8,128)(2,1)}) %tuple.249), branch_computations={%region_1.1_spmd, %region_2.4_spmd} | conditional | flops 849264768 | bytes 10868772 | solution.py:156
  237.4 2.9 fusion.228
  243.4 3.3 fusion.3
  246.6 4.5 collective-permute-start
  256.1 14.7 %conditional.5 = (bf16[2,8,8,640]{3,2,1,0:T(8,128)(2,1)S(1)}) conditional(s32[]{:T(128)} %convert_element_type.191, () %tuple.248, (bf16[2,8,8,640]{3,2,1,0:T(8,128)(2,1)}, f32[49,640]{1,0:T(8,128)}, bf16[640,2560]{1,0:T(8,128)(2,1)S(1)}, bf16[2560,640]{1,0:T(8,128)(2,1)}) %tuple.249), branch_computations={%region_1.1_spmd, %region_2.4_spmd} | conditional | flops 849264768 | bytes 10868772 | solution.py:156
  261.6 2.9 fusion.228
  267.5 3.3 fusion.3
  270.8 4.5 collective-permute-start
  280.3 14.7 %conditional.5 = (bf16[2,8,8,640]{3,2,1,0:T(8,128)(2,1)S(1)}) conditional(s32[]{:T(128)} %convert_element_type.191, () %tuple.248, (bf16[2,8,8,640]{3,2,1,0:T(8,128)(2,1)}, f32[49,640]{1,0:T(8,128)}, bf16[640,2560]{1,0:T(8,128)(2,1)S(1)}, bf16[2560,640]{1,0:T(8,128)(2,1)}) %tuple.249), branch_computations={%region_1.1_spmd, %region_2.4_spmd} | conditional | flops 849264768 | bytes 10868772 | solution.py:156
  291.7 3.3 fusion.3
  295.0 4.5 collective-permute-start
  304.5 19.2 %collective-permute-start = (bf16[2,8,8,640]{3,2,1,0:T(8,128)(2,1)S(1)}, bf16[2,8,8,640]{3,2,1,0:T(8,128)(2,1)}, u32[]{:S(2)}, u32[]{:S(2)}) collective-permute-start(bf16[2,8,8,640]{3,2,1,0:T(8,128)(2,1)S(1)} %get-tuple-element.1153), channel_id=1, source_target_pairs={{0,32},{32,64},{64,96},{96,128},{128,160},{160,192},{192,224},{1,3... | collective-permute-start | bytes 491528 | tf_op jit(solution)/shard_map/while/body/eval_jaxpr/ppermute | solution.py:22
  328.7 4.5 collective-permute-start
  338.2 12.7 collective-permute-start
  355.9 4.5 collective-permute-start
  365.5 16.6 %collective-permute-start = (bf16[2,8,8,640]{3,2,1,0:T(8,128)(2,1)S(1)}, bf16[2,8,8,640]{3,2,1,0:T(8,128)(2,1)}, u32[]{:S(2)}, u32[]{:S(2)}) collective-permute-start(bf16[2,8,8,640]{3,2,1,0:T(8,128)(2,1)S(1)} %get-tuple-element.1153), channel_id=1, source_target_pairs={{0,32},{32,64},{64,96},{96,128},{128,160},{160,192},{192,224},{1,3... | collective-permute-start | bytes 491528 | tf_op jit(solution)/shard_map/while/body/eval_jaxpr/ppermute | solution.py:22
  387.1 4.5 collective-permute-start
  396.5 3.1 broadcast_in_dim.54
  399.7 3.5 broadcast_in_dim.53
  403.2 778.2 %while.41 = (s32[]{:T(128)}, bf16[2,8,8,640]{3,2,1,0:T(8,128)(2,1)}, f32[49,640]{1,0:T(8,128)S(1)}, f32[640,2560]{1,0:T(8,128)}, f32[2560,640]{1,0:T(8,128)}, /*...) while((s32[]{:T(128)}, ...), condition=%wide.region_63.64_spmd.clone, body=%wide.region_7.63_spmd.clone.sunk | while | flops 2131804288 | bytes 130983528 | solution.py:220
  407.5 14.1 collective-permute-done.1
  425.9 5.0 collective-permute-done.1
  435.2 17.3 %collective-permute-done.1 = bf16[2,8,8,640]{3,2,1,0:T(8,128)(2,1)} collective-permute-done((bf16[2,8,8,640]{3,2,1,0:T(8,128)(2,1)}, bf16[2,8,8,640]{3,2,1,0:T(8,128)(2,1)}, u32[]{:S(2)}, u32[]{:S(2)}) %collective-permute-start.1) | collective-permute-done | bytes 163872 | tf_op jit(solution)/shard_map/while/body/eval_jaxpr/ppermute | solution.py:22
  456.8 5.0 collective-permute-done.1
  466.1 13.4 collective-permute-done.1
  483.8 359.0 %collective-permute-done.1 = bf16[2,8,8,640]{3,2,1,0:T(8,128)(2,1)} collective-permute-done((bf16[2,8,8,640]{3,2,1,0:T(8,128)(2,1)}, bf16[2,8,8,640]{3,2,1,0:T(8,128)(2,1)}, u32[]{:S(2)}, u32[]{:S(2)}) %collective-permute-start.1) | collective-permute-done | bytes 163872 | tf_op jit(solution)/shard_map/while/body/eval_jaxpr/ppermute | solution.py:22
  844.6 60.5 %conditional.6 = (bf16[2,8,8,640]{3,2,1,0:T(8,128)(2,1)}, f32[49,640]{1,0:T(8,128)S(1)}, f32[640,2560]{1,0:T(8,128)}, f32[2560,640]{1,0:T(8,128)}) conditional(s32[]{:T(128)} %convert_element_type.193, (f32[49,640]{1,0:T(8,128)S(1)}, f32[640,2560]{1,0:T(8,128)}, f32[2560,640]{1,0:T(8,128)}) %tuple.251, (pred[]{:T(512)}, s32[]{:T(128)}, ...), branch_computations={%region_8.8_spmd, %region_9.62_spmd} | conditional | flops 2131148928 | bytes 129667864 | solution.py:214
  848.7 2.9 fusion.230
  884.0 8.0 stack.299
  893.8 7.2 convolution_add_fusion.1
  906.9 5.0 collective-permute-done.1
  913.7 60.5 %conditional.6 = (bf16[2,8,8,640]{3,2,1,0:T(8,128)(2,1)}, f32[49,640]{1,0:T(8,128)S(1)}, f32[640,2560]{1,0:T(8,128)}, f32[2560,640]{1,0:T(8,128)}) conditional(s32[]{:T(128)} %convert_element_type.193, (f32[49,640]{1,0:T(8,128)S(1)}, f32[640,2560]{1,0:T(8,128)}, f32[2560,640]{1,0:T(8,128)}) %tuple.251, (pred[]{:T(512)}, s32[]{:T(128)}, ...), branch_computations={%region_8.8_spmd, %region_9.62_spmd} | conditional | flops 2131148928 | bytes 129667864 | solution.py:214
  917.8 2.9 fusion.230
  953.1 8.0 stack.299
  962.9 7.2 convolution_add_fusion.1
  976.0 5.0 collective-permute-done.1
  982.8 60.5 %conditional.6 = (bf16[2,8,8,640]{3,2,1,0:T(8,128)(2,1)}, f32[49,640]{1,0:T(8,128)S(1)}, f32[640,2560]{1,0:T(8,128)}, f32[2560,640]{1,0:T(8,128)}) conditional(s32[]{:T(128)} %convert_element_type.193, (f32[49,640]{1,0:T(8,128)S(1)}, f32[640,2560]{1,0:T(8,128)}, f32[2560,640]{1,0:T(8,128)}) %tuple.251, (pred[]{:T(512)}, s32[]{:T(128)}, ...), branch_computations={%region_8.8_spmd, %region_9.62_spmd} | conditional | flops 2131148928 | bytes 129667864 | solution.py:214
  986.9 2.9 fusion.230
  1022.2 8.0 stack.299
  1032.0 7.2 convolution_add_fusion.1
  1045.1 5.0 collective-permute-done.1
  1051.9 60.5 %conditional.6 = (bf16[2,8,8,640]{3,2,1,0:T(8,128)(2,1)}, f32[49,640]{1,0:T(8,128)S(1)}, f32[640,2560]{1,0:T(8,128)}, f32[2560,640]{1,0:T(8,128)}) conditional(s32[]{:T(128)} %convert_element_type.193, (f32[49,640]{1,0:T(8,128)S(1)}, f32[640,2560]{1,0:T(8,128)}, f32[2560,640]{1,0:T(8,128)}) %tuple.251, (pred[]{:T(512)}, s32[]{:T(128)}, ...), branch_computations={%region_8.8_spmd, %region_9.62_spmd} | conditional | flops 2131148928 | bytes 129667864 | solution.py:214
  1056.0 2.9 fusion.230
  1091.3 8.0 stack.299
  1101.1 7.2 convolution_add_fusion.1
  1114.2 5.0 collective-permute-done.1
  1121.6 58.4 %collective-permute-start.1 = (bf16[2,8,8,640]{3,2,1,0:T(8,128)(2,1)}, bf16[2,8,8,640]{3,2,1,0:T(8,128)(2,1)}, u32[]{:S(2)}, u32[]{:S(2)}) collective-permute-start(bf16[2,8,8,640]{3,2,1,0:T(8,128)(2,1)} %get-tuple-element.1051), channel_id=1, source_target_pairs={{32,0},{64,32},{96,64},{128,96},{160,128},{192,160},{224,192},{33,... | collective-permute-start | bytes 491528 | tf_op jit(solution)/shard_map/while/body/eval_jaxpr/ppermute | solution.py:22
  1182.1 4.9 convert_element_type.148
  1188.8 3.2 convert_element_type.147
  1192.1 81.5 %fusion.2 = bf16[24,2560]{1,0:T(8,128)(2,1)S(1)} fusion(bf16[640,2560]{1,0:T(8,128)(2,1)S(1)} %convert_element_type.147), kind=kCustom, calls=%all-reduce-scatter | all-reduce-scatter fusion | flops 1966081 | bytes 3400704
  1277.7 6.0 collective-permute-start.5
  1283.8 4.6 collective-permute-start.4
  1288.4 5.6 collective-permute-start.3
  1296.2 85.4 %all-reduce.5 = (f32[640]{0:T(1024)}, f32[]{:T(128)}) all-reduce(f32[640]{0:T(1024)S(1)} %broadcast_multiply_fusion.4, f32[]{:T(128)S(6)} %mul.2377), channel_id=1, replica_groups=mesh['section'=8,'dp'=32] {'section','dp'}, use_global_device_ids=true, to_apply=%region_68.69 | all-reduce | flops 641 | bytes 5128 | tf_op jit(solution)/shard_map/psum | solution.py:180
  1386.7 69.0 %reduce-scatter.4.cloned.1.call-done = bf16[80,640]{1,0:T(8,128)(2,1)} async-done(((bf16[2560,640]{1,0:T(8,128)(2,1)}), bf16[80,640]{1,0:T(8,128)(2,1)}) %reduce-scatter.4.cloned.1.call-update) | async-done | bytes 102416 | tf_op jit(solution)/shard_map/reduce_scatter | solution.py:227
  (1136 shorter events, 331.5 us)
Async XLA Ops:
  7.2 5.0 copy-start.76
  7.2 97.2 %all-gather.8.cloned.1.call-start = ((), (), s32[]{:S(2)}) async-start(), calls=%async_computation.2 | async-start | bytes 6758400 | tf_op jit(solution)/shard_map/all_gather | solution.py:143
  9.0 171.6 %all-gather.10.cloned.1.call-start = ((), (), s32[]{:S(2)}) async-start(), calls=%async_computation.3 | async-start | bytes 3379200 | tf_op jit(solution)/shard_map/all_gather | solution.py:144
  9.8 1374.2 %all-gather.12.cloned.1.call-start = ((), (), s32[]{:S(2)}) async-start(), calls=%async_computation.4 | async-start | bytes 2365440 | tf_op jit(solution)/shard_map/all_gather | solution.py:13
  183.2 212.0 %copy-start.80 = (s32[1,4,2,8,8]{4,3,2,1,0:T(8,128)S(1)}, s32[1,4,2,8,8]{4,3,2,1,0:T(8,128)}, u32[]{:S(2)}) copy-start(s32[1,4,2,8,8]{4,3,2,1,0:T(8,128)} %param.16) | copy-start | bytes 6148
  185.9 21.6 %collective-permute-start = (bf16[2,8,8,640]{3,2,1,0:T(8,128)(2,1)S(1)}, bf16[2,8,8,640]{3,2,1,0:T(8,128)(2,1)}, u32[]{:S(2)}, u32[]{:S(2)}) collective-permute-start(bf16[2,8,8,640]{3,2,1,0:T(8,128)(2,1)S(1)} %get-tuple-element.1153), channel_id=1, source_target_pairs={{0,32},{32,64},{64,96},{96,128},{128,160},{160,192},{192,224},{1,3... | collective-permute-start | bytes 491528 | tf_op jit(solution)/shard_map/while/body/eval_jaxpr/ppermute | solution.py:22
  225.0 4.2 collective-permute-start
  246.6 6.8 collective-permute-start
  270.8 6.7 collective-permute-start
  295.0 6.7 collective-permute-start
  304.5 21.4 %collective-permute-start = (bf16[2,8,8,640]{3,2,1,0:T(8,128)(2,1)S(1)}, bf16[2,8,8,640]{3,2,1,0:T(8,128)(2,1)}, u32[]{:S(2)}, u32[]{:S(2)}) collective-permute-start(bf16[2,8,8,640]{3,2,1,0:T(8,128)(2,1)S(1)} %get-tuple-element.1153), channel_id=1, source_target_pairs={{0,32},{32,64},{64,96},{96,128},{128,160},{160,192},{192,224},{1,3... | collective-permute-start | bytes 491528 | tf_op jit(solution)/shard_map/while/body/eval_jaxpr/ppermute | solution.py:22
  328.7 6.7 collective-permute-start
  338.2 14.9 %collective-permute-start = (bf16[2,8,8,640]{3,2,1,0:T(8,128)(2,1)S(1)}, bf16[2,8,8,640]{3,2,1,0:T(8,128)(2,1)}, u32[]{:S(2)}, u32[]{:S(2)}) collective-permute-start(bf16[2,8,8,640]{3,2,1,0:T(8,128)(2,1)S(1)} %get-tuple-element.1153), channel_id=1, source_target_pairs={{0,32},{32,64},{64,96},{96,128},{128,160},{160,192},{192,224},{1,3... | collective-permute-start | bytes 491528 | tf_op jit(solution)/shard_map/while/body/eval_jaxpr/ppermute | solution.py:22
  355.9 6.7 collective-permute-start
  365.5 18.8 %collective-permute-start = (bf16[2,8,8,640]{3,2,1,0:T(8,128)(2,1)S(1)}, bf16[2,8,8,640]{3,2,1,0:T(8,128)(2,1)}, u32[]{:S(2)}, u32[]{:S(2)}) collective-permute-start(bf16[2,8,8,640]{3,2,1,0:T(8,128)(2,1)S(1)} %get-tuple-element.1153), channel_id=1, source_target_pairs={{0,32},{32,64},{64,96},{96,128},{128,160},{160,192},{192,224},{1,3... | collective-permute-start | bytes 491528 | tf_op jit(solution)/shard_map/while/body/eval_jaxpr/ppermute | solution.py:22
  387.1 6.7 collective-permute-start
  405.6 16.0 %collective-permute-start.1 = (bf16[2,8,8,640]{3,2,1,0:T(8,128)(2,1)}, bf16[2,8,8,640]{3,2,1,0:T(8,128)(2,1)}, u32[]{:S(2)}, u32[]{:S(2)}) collective-permute-start(bf16[2,8,8,640]{3,2,1,0:T(8,128)(2,1)} %get-tuple-element.1051), channel_id=1, source_target_pairs={{32,0},{64,32},{96,64},{128,96},{160,128},{192,160},{224,192},{33,... | collective-permute-start | bytes 491528 | tf_op jit(solution)/shard_map/while/body/eval_jaxpr/ppermute | solution.py:22
  423.9 6.9 collective-permute-start.1
  433.3 19.2 %collective-permute-start.1 = (bf16[2,8,8,640]{3,2,1,0:T(8,128)(2,1)}, bf16[2,8,8,640]{3,2,1,0:T(8,128)(2,1)}, u32[]{:S(2)}, u32[]{:S(2)}) collective-permute-start(bf16[2,8,8,640]{3,2,1,0:T(8,128)(2,1)} %get-tuple-element.1051), channel_id=1, source_target_pairs={{32,0},{64,32},{96,64},{128,96},{160,128},{192,160},{224,192},{33,... | collective-permute-start | bytes 491528 | tf_op jit(solution)/shard_map/while/body/eval_jaxpr/ppermute | solution.py:22
  454.9 6.9 collective-permute-start.1
  464.2 15.3 %collective-permute-start.1 = (bf16[2,8,8,640]{3,2,1,0:T(8,128)(2,1)}, bf16[2,8,8,640]{3,2,1,0:T(8,128)(2,1)}, u32[]{:S(2)}, u32[]{:S(2)}) collective-permute-start(bf16[2,8,8,640]{3,2,1,0:T(8,128)(2,1)} %get-tuple-element.1051), channel_id=1, source_target_pairs={{32,0},{64,32},{96,64},{128,96},{160,128},{192,160},{224,192},{33,... | collective-permute-start | bytes 491528 | tf_op jit(solution)/shard_map/while/body/eval_jaxpr/ppermute | solution.py:22
  481.9 361.0 %collective-permute-start.1 = (bf16[2,8,8,640]{3,2,1,0:T(8,128)(2,1)}, bf16[2,8,8,640]{3,2,1,0:T(8,128)(2,1)}, u32[]{:S(2)}, u32[]{:S(2)}) collective-permute-start(bf16[2,8,8,640]{3,2,1,0:T(8,128)(2,1)} %get-tuple-element.1051), channel_id=1, source_target_pairs={{32,0},{64,32},{96,64},{128,96},{160,128},{192,160},{224,192},{33,... | collective-permute-start | bytes 491528 | tf_op jit(solution)/shard_map/while/body/eval_jaxpr/ppermute | solution.py:22
  848.2 3.5 copy-start.14
  860.9 3.7 copy-start.3
  864.6 19.4 %copy-start.77 = (f32[1,640]{1,0:T(1,128)S(1)}, f32[1,640]{1,0:T(1,128)}, u32[]{:S(2)}) copy-start(f32[1,640]{1,0:T(1,128)} %stack.274) | copy-start | bytes 7684 | tf_op jit(solution)/shard_map/while/body/eval_jaxpr/cond
  892.0 9.0 slice-start
  893.8 7.2 slice-start.1
  893.8 7.2 copy-start.6
  893.8 7.2 copy-start.8
  901.0 4.1 copy-start.13
  905.0 6.9 collective-permute-start.1
  930.0 3.7 copy-start.3
  933.7 19.4 %copy-start.77 = (f32[1,640]{1,0:T(1,128)S(1)}, f32[1,640]{1,0:T(1,128)}, u32[]{:S(2)}) copy-start(f32[1,640]{1,0:T(1,128)} %stack.274) | copy-start | bytes 7684 | tf_op jit(solution)/shard_map/while/body/eval_jaxpr/cond
  961.1 9.0 slice-start
  962.9 7.2 slice-start.1
  962.9 7.2 copy-start.6
  962.9 7.2 copy-start.8
  970.1 4.1 copy-start.13
  974.1 6.9 collective-permute-start.1
  986.4 3.5 copy-start.14
  999.1 3.7 copy-start.3
  1002.8 19.4 %copy-start.77 = (f32[1,640]{1,0:T(1,128)S(1)}, f32[1,640]{1,0:T(1,128)}, u32[]{:S(2)}) copy-start(f32[1,640]{1,0:T(1,128)} %stack.274) | copy-start | bytes 7684 | tf_op jit(solution)/shard_map/while/body/eval_jaxpr/cond
  1030.2 9.0 slice-start
  1032.0 7.2 slice-start.1
  1032.0 7.2 copy-start.6
  1032.0 7.2 copy-start.8
  1039.1 4.1 copy-start.13
  1043.2 6.9 collective-permute-start.1
  1068.2 3.7 copy-start.3
  1071.9 19.4 %copy-start.77 = (f32[1,640]{1,0:T(1,128)S(1)}, f32[1,640]{1,0:T(1,128)}, u32[]{:S(2)}) copy-start(f32[1,640]{1,0:T(1,128)} %stack.274) | copy-start | bytes 7684 | tf_op jit(solution)/shard_map/while/body/eval_jaxpr/cond
  1099.2 9.0 slice-start
  1101.0 7.2 slice-start.1
  1101.0 7.2 copy-start.6
  1101.1 7.2 copy-start.8
  1108.2 4.1 copy-start.13
  1112.3 6.9 collective-permute-start.1
  1121.6 59.7 %collective-permute-start.1 = (bf16[2,8,8,640]{3,2,1,0:T(8,128)(2,1)}, bf16[2,8,8,640]{3,2,1,0:T(8,128)(2,1)}, u32[]{:S(2)}, u32[]{:S(2)}) collective-permute-start(bf16[2,8,8,640]{3,2,1,0:T(8,128)(2,1)} %get-tuple-element.1051), channel_id=1, source_target_pairs={{32,0},{64,32},{96,64},{128,96},{160,128},{192,160},{224,192},{33,... | collective-permute-start | bytes 491528 | tf_op jit(solution)/shard_map/while/body/eval_jaxpr/ppermute | solution.py:22
  1182.0 273.6 %reduce-scatter.4.cloned.1.call-start = ((), (), s32[]{:S(2)}) async-start(), calls=%async_computation.1 | async-start | bytes 3379200 | tf_op jit(solution)/shard_map/reduce_scatter | solution.py:227
  1273.6 21.0 %collective-permute-start.7 = (bf16[4,2560]{1,0:T(4,128)(2,1)S(1)}, bf16[4,2560]{1,0:T(4,128)(2,1)S(1)}, u32[]{:S(2)}, u32[]{:S(2)}) collective-permute-start(bf16[4,2560]{1,0:T(4,128)(2,1)S(1)} %slice.1262), channel_id=1, source_target_pairs={{0,6},{1,7},{2,8},{3,9},{4,10},{5,11},{6,12},{7,13},{8,14},{9,15},... | collective-permute-start | bytes 61448
  1276.4 105.2 %collective-permute-start.6 = (bf16[24,2560]{1,0:T(8,128)(2,1)S(1)}, bf16[24,2560]{1,0:T(8,128)(2,1)S(1)}, u32[]{:S(2)}, u32[]{:S(2)}) collective-permute-start(bf16[24,2560]{1,0:T(8,128)(2,1)S(1)} %fusion.2), channel_id=1, source_target_pairs={{0,5},{1,6},{2,7},{3,8},{4,9},{5,10},{6,11},{7,12},{8,13},{9,14},{... | collective-permute-start | bytes 368648
  1277.7 103.9 %collective-permute-start.5 = (bf16[24,2560]{1,0:T(8,128)(2,1)S(1)}, bf16[24,2560]{1,0:T(8,128)(2,1)S(1)}, u32[]{:S(2)}, u32[]{:S(2)}) collective-permute-start(bf16[24,2560]{1,0:T(8,128)(2,1)S(1)} %fusion.2), channel_id=1, source_target_pairs={{0,4},{1,5},{2,6},{3,7},{4,8},{5,9},{6,10},{7,11},{8,12},{9,13},{1... | collective-permute-start | bytes 368648
  1283.8 97.9 %collective-permute-start.4 = (bf16[24,2560]{1,0:T(8,128)(2,1)S(1)}, bf16[24,2560]{1,0:T(8,128)(2,1)S(1)}, u32[]{:S(2)}, u32[]{:S(2)}) collective-permute-start(bf16[24,2560]{1,0:T(8,128)(2,1)S(1)} %fusion.2), channel_id=1, source_target_pairs={{0,3},{1,4},{2,5},{3,6},{4,7},{5,8},{6,9},{7,10},{8,11},{9,12},{10... | collective-permute-start | bytes 368648
  1288.4 93.3 %collective-permute-start.3 = (bf16[24,2560]{1,0:T(8,128)(2,1)S(1)}, bf16[24,2560]{1,0:T(8,128)(2,1)S(1)}, u32[]{:S(2)}, u32[]{:S(2)}) collective-permute-start(bf16[24,2560]{1,0:T(8,128)(2,1)S(1)} %fusion.2), channel_id=1, source_target_pairs={{0,2},{1,3},{2,4},{3,5},{4,6},{5,7},{6,8},{7,9},{8,10},{9,11},{10,... | collective-permute-start | bytes 368648
  1294.6 87.0 %collective-permute-start.2 = (bf16[24,2560]{1,0:T(8,128)(2,1)S(1)}, bf16[24,2560]{1,0:T(8,128)(2,1)S(1)}, u32[]{:S(2)}, u32[]{:S(2)}) collective-permute-start(bf16[24,2560]{1,0:T(8,128)(2,1)S(1)} %fusion.2), channel_id=1, source_target_pairs={{0,1},{1,2},{2,3},{3,4},{4,5},{5,6},{6,7},{7,8},{8,9},{9,10},{10,1... | collective-permute-start | bytes 368648
  (299 other events, 619.8 us)
Sparse Core Ops, SparseCore 0:
  11.2 93.1 all-gather.7
  107.0 73.6 all-gather.9
  1182.1 73.3 all-gather.11
  1259.2 196.3 reduce-scatter.3
